TPU v7x, 32 devices: a whole 2x2x4 slice. The times are simulated.
32 devices in a mesh: dp: 4 (over y, x), seq: 8 (over z, core).
Axes of the slice: x: 2, y: 2, z: 4, core: 2. Of those that a mesh axis runs over, the one named last changes fastest.
Arguments:
- tokens: float32 [4, 1024, 1024], P('dp', 'seq'), may hold values from -6 to 6
- cotangent: float32 [4, 1024, 1024], P('dp', 'seq'), may hold values from -6 to 6
- doc_ids: int32 [4, 1024], P('dp'), may hold values from 0 to 1, never falling along the last dimension, each value on 1 to 768 neighbouring positions
- in_weight: float32 [1024, 4384], P(('dp', 'seq')), may hold values from -0.1875 to 0.1875
- out_weight: float32 [1024, 2048], P(('dp', 'seq')), may hold values from -0.125 to 0.125
- in_m: float32 [1024, 4384], P(('dp', 'seq')), may hold values from -30 to 30
- in_v: float32 [1024, 4384], P(('dp', 'seq')), may hold values from 1 to 1000
- out_m: float32 [1024, 2048], P(('dp', 'seq')), may hold values from -30 to 30
- out_v: float32 [1024, 2048], P(('dp', 'seq')), may hold values from 1 to 1000
- vec_params: float32 [14688], replicated, as said below
- vec_m: float32 [14688], replicated, may hold values from -30 to 30
- vec_v: float32 [14688], replicated, may hold values from 1 to 1000
Outputs:
- activations: float32 [4, 1024, 1024], P('dp', 'seq')
- input_grad: float32 [4, 1024, 1024], P('dp', 'seq')
- in_grad: float32 [1024, 4384], P(('dp', 'seq'))
- out_grad: float32 [1024, 2048], P(('dp', 'seq'))
- vec_grad: float32 [14688], replicated
- in_new: float32 [1024, 4384], P(('dp', 'seq'))
- out_new: float32 [1024, 2048], P(('dp', 'seq'))
- vec_new: float32 [14688], replicated
- in_m_new: float32 [1024, 4384], P(('dp', 'seq'))
- in_v_new: float32 [1024, 4384], P(('dp', 'seq'))
- out_m_new: float32 [1024, 2048], P(('dp', 'seq'))
- out_v_new: float32 [1024, 2048], P(('dp', 'seq'))
- vec_m_new: float32 [14688], replicated
- vec_v_new: float32 [14688], replicated
Inputs may be any that keep to these rules, and one draw needn't show every extreme that they name: `doc_ids`: each row holds document 0 and then document 1, each of one or more positions, none longer than 768. `vec_params`: norm_gain and gate_gain lie in 0.7 to 1.3, skip_gain in 0.5 to 1.5, step_bias in -1 to 1, log_rate in -12 to -3.
All inputs are finite; a program needn't handle non-finite values.
Results may differ from a plain program's by a relative error of at most 0.015.
Values may be sent and summed in bfloat16 or wider, within the bound.
A program may use at most 192 MiB of HBM per device.

v0:
```python
import jax
import jax.numpy as jnp
from jax import lax
from jax.sharding import PartitionSpec as P

D = 1024
DI = 2048
H = 32
P_SIZE = 64
N = 128
KW = 4
STRETCH = 256
STEP = 10
CONV = 2304
norm_eps = 1e-05
beta_one = 0.9
beta_two = 0.95
learn_rate = 0.03
decay_rate = 0.1
adam_eps = 1e-08
top_precision = lax.Precision.HIGHEST


def shifted_2(block, axis, distance):
    devices = range(lax.axis_size(axis))
    route = [(i - distance, i) for i in devices if i - distance in devices]
    return lax.ppermute(block, axis, route)


def unpack(vector):
    cursor = D + DI
    norm_gain = vector[:D]
    gate_gain = vector[D:cursor]
    conv_kernel = vector[cursor : cursor + KW * CONV].reshape(KW, CONV)
    cursor = cursor + KW * CONV
    conv_bias = vector[cursor : cursor + CONV]
    cursor = cursor + CONV
    step_bias = vector[cursor : cursor + H]
    log_rate = vector[cursor + H : cursor + 2 * H]
    skip_gain = vector[cursor + 2 * H : cursor + 3 * H]
    return (norm_gain, gate_gain, conv_kernel, conv_bias, step_bias, log_rate, skip_gain)


def repack(norm_gain, gate_gain, conv_kernel, conv_bias, step_bias, log_rate, skip_gain):
    return jnp.concatenate(
        [norm_gain, gate_gain, conv_kernel.reshape(-1), conv_bias, step_bias, log_rate, skip_gain]
    )


def input_norm(inputs, gain):
    scale = lax.rsqrt(jnp.mean(inputs * inputs, axis=-1, keepdims=True) + norm_eps)
    return inputs * scale * gain[None, :]


def gate_norm(ssd_out, gate_in, gain):
    mixed = ssd_out * jax.nn.silu(gate_in)
    scale = lax.rsqrt(jnp.mean(mixed * mixed, axis=-1, keepdims=True) + norm_eps)
    return mixed * scale * gain[None, :]


def conv_silu(padded, conv_kernel, conv_bias, ext_ids):
    length = padded.shape[0] - (KW - 1)
    own_ids = ext_ids[KW - 1 :]
    total = jnp.zeros((length, padded.shape[1]), jnp.float32) + conv_bias[None, :]
    for offset in range(KW):
        valid = (ext_ids[offset : offset + length] == own_ids).astype(jnp.float32)
        total = (
            total + conv_kernel[offset][None, :] * padded[offset : offset + length] * valid[:, None]
        )
    return jax.nn.silu(total)


def rates(step_raw, step_bias, log_rate):
    step_size = jax.nn.softplus(step_raw + step_bias[None, :])
    log_decay = -jnp.exp(log_rate)[None, :] * step_size
    return (step_size, log_decay)


def ssd_block(state, pieces):
    values, input_map, output_map, step_size, log_decay, block_ids, prior_id = pieces
    length = values.shape[0]
    cumulative = jnp.cumsum(log_decay, axis=0)
    rows_index = lax.broadcasted_iota(jnp.int32, (length, length), 0)
    cols_index = lax.broadcasted_iota(jnp.int32, (length, length), 1)
    related = (block_ids[:, None] == block_ids[None, :]) & (rows_index >= cols_index)
    spans = cumulative.T[:, :, None] - cumulative.T[:, None, :]
    decays = jnp.where(related[None], jnp.exp(jnp.where(related[None], spans, 0.0)), 0.0)
    scores = jnp.dot(output_map, input_map.T, precision=top_precision)
    mixing = decays * scores[None] * step_size.T[:, None, :]
    inside = jnp.einsum("hij,jhp->ihp", mixing, values, precision=top_precision)
    carried = (block_ids == prior_id).astype(jnp.float32)
    reach = carried[:, None] * jnp.exp(cumulative)
    entering = (
        jnp.einsum("hpn,in->ihp", state, output_map, precision=top_precision) * reach[:, :, None]
    )
    ending = (block_ids == block_ids[-1]).astype(jnp.float32)
    tail_weight = ending[:, None] * jnp.exp(cumulative[-1][None, :] - cumulative) * step_size
    new_state = state * reach[-1][:, None, None] + jnp.einsum(
        "jh,jhp,jn->hpn", tail_weight, values, input_map, precision=top_precision
    )
    return (new_state, inside + entering)


def ssd_run(mixed_in, step_size, log_decay, skip_gain, row_ids, prior_id, state, block):
    length = mixed_in.shape[0]
    blocks = length // block
    values = mixed_in[:, :DI].reshape(length, H, P_SIZE)
    input_map = mixed_in[:, DI : DI + N]
    output_map = mixed_in[:, DI + N :]
    shifted = jnp.concatenate([jnp.reshape(prior_id, (1,)), row_ids[:-1]])
    priors = shifted.reshape(blocks, block)[:, 0]
    pieces = (
        values.reshape(blocks, block, H, P_SIZE),
        input_map.reshape(blocks, block, N),
        output_map.reshape(blocks, block, N),
        step_size.reshape(blocks, block, H),
        log_decay.reshape(blocks, block, H),
        row_ids.reshape(blocks, block),
        priors,
    )
    final, outputs = lax.scan(ssd_block, state, pieces)
    result = outputs.reshape(length, H, P_SIZE) + skip_gain[None, :, None] * values
    return (result.reshape(length, DI), final)


def adamw_update(param, grad, first, second):
    first_new = beta_one * first + (1.0 - beta_one) * grad
    second_new = beta_two * second + (1.0 - beta_two) * grad * grad
    corrected = first_new / (1.0 - beta_one**STEP)
    scaled = jnp.sqrt(second_new / (1.0 - beta_two**STEP)) + adam_eps
    return (
        param * (1.0 - learn_rate * decay_rate) - learn_rate * corrected / scaled,
        first_new,
        second_new,
    )


def body(
    tokens,
    cotangent,
    doc_ids,
    in_weight,
    out_weight,
    in_m,
    in_v,
    out_m,
    out_v,
    vec_params,
    vec_m,
    vec_v,
):
    in_work, out_work = (
        lax.all_gather(in_weight.astype(jnp.bfloat16), ("dp", "seq"), axis=0, tiled=True),
        lax.all_gather(out_weight.astype(jnp.bfloat16), ("dp", "seq"), axis=0, tiled=True),
    )
    norm_gain, gate_gain, conv_kernel, conv_bias, step_bias, log_rate, skip_gain = unpack(
        vec_params
    )
    inputs = tokens[0]
    upstream_f = cotangent[0]
    local_len = inputs.shape[0]
    block = min(STRETCH, local_len)
    padded_row = jnp.concatenate([jnp.full((KW - 1,), -1, jnp.int32), doc_ids[0]])
    offset = lax.axis_index("seq") * local_len
    ext_ids = lax.dynamic_slice_in_dim(padded_row, offset, local_len + KW - 1)
    own_ids = ext_ids[KW - 1 :]
    prior_id = ext_ids[KW - 2]
    zero_state = jnp.zeros((H, P_SIZE, N), jnp.float32)
    normed = input_norm(inputs, norm_gain).astype(jnp.bfloat16)
    projected = jnp.dot(normed, in_work, preferred_element_type=jnp.float32)
    gate_in = projected[:, :DI]
    conv_in = projected[:, DI : DI + CONV].astype(jnp.bfloat16)
    step_raw = projected[:, DI + CONV :]
    rim = shifted_2(conv_in[local_len - (KW - 1) :], "seq", 1)
    padded = lax.optimization_barrier(jnp.concatenate([rim, conv_in], axis=0)).astype(jnp.float32)
    mixed_in = lax.optimization_barrier(
        conv_silu(padded, conv_kernel, conv_bias, ext_ids).astype(jnp.bfloat16)
    ).astype(jnp.float32)
    output_map = mixed_in[:, DI + N :]

    def pre_chain(mixed, raw, bias_in, rate_in, skip_in):
        step_size, log_decay = rates(raw, bias_in, rate_in)
        local_out, local_state = ssd_run(
            mixed, step_size, log_decay, skip_in, own_ids, prior_id, zero_state, block
        )
        cumulative = jnp.cumsum(log_decay, axis=0)
        reach = (own_ids == prior_id).astype(jnp.float32)[:, None] * jnp.exp(cumulative)
        return (local_out, local_state, reach)

    local_out, local_state, reach = pre_chain(mixed_in, step_raw, step_bias, log_rate, skip_gain)
    decay = reach[-1]

    def relay(turn, entry_now):
        return shifted_2(decay[:, None, None] * entry_now + local_state, "seq", 1)

    entry = lax.fori_loop(0, lax.axis_size("seq") - 1, relay, zero_state)
    entering = (
        jnp.einsum("hpn,tn->thp", entry, output_map, precision=top_precision) * reach[:, :, None]
    )
    ssd_out = local_out + entering.reshape(local_len, DI)
    gated, gate_back = jax.vjp(gate_norm, ssd_out, gate_in, gate_gain)
    normed_out = gated.astype(jnp.bfloat16)
    outputs = inputs + lax.dot_general(
        normed_out, out_work, (((1,), (1,)), ((), ())), preferred_element_type=jnp.float32
    )
    upstream = upstream_f.astype(jnp.bfloat16)
    grad_gated = jnp.dot(upstream, out_work, preferred_element_type=jnp.float32)
    grad_ssd, grad_gate_in, grad_gate_gain = gate_back(grad_gated)
    own_part = jnp.einsum(
        "th,thp,tn->hpn",
        reach,
        grad_ssd.reshape(local_len, H, P_SIZE),
        output_map,
        precision=top_precision,
    )

    def back_relay(turn, later):
        return shifted_2(
            (own_part + decay[:, None, None] * later).astype(jnp.bfloat16), "seq", -1
        ).astype(jnp.float32)

    after = lax.fori_loop(0, lax.axis_size("seq") - 1, back_relay, zero_state)

    def complete(mixed, raw, bias_in, rate_in, skip_in):
        part_out, part_state, part_reach = pre_chain(mixed, raw, bias_in, rate_in, skip_in)
        reader = mixed[:, DI + N :]
        arriving = (
            jnp.einsum("hpn,tn->thp", entry, reader, precision=top_precision)
            * part_reach[:, :, None]
        )
        return (part_out + arriving.reshape(local_len, DI), part_reach[-1], part_state)

    _, ssd_back = jax.vjp(complete, mixed_in, step_raw, step_bias, log_rate, skip_gain)
    grad_mixed, grad_raw, grad_bias, grad_rate, grad_skip = ssd_back(
        (grad_ssd, jnp.sum(after * entry, axis=(1, 2)), after)
    )
    _, conv_back = jax.vjp(
        lambda values, kernel, constant: conv_silu(values, kernel, constant, ext_ids),
        padded,
        conv_kernel,
        conv_bias,
    )
    grad_padded, grad_kernel, grad_cbias = conv_back(grad_mixed)
    returned = shifted_2(grad_padded[: KW - 1], "seq", -1)
    grad_conv = jnp.concatenate(
        [grad_padded[KW - 1 : local_len], grad_padded[local_len:] + returned], axis=0
    )
    grad_proj = jnp.concatenate([grad_gate_in, grad_conv, grad_raw], axis=1).astype(jnp.bfloat16)
    grad_normed = lax.dot_general(
        grad_proj, in_work, (((1,), (1,)), ((), ())), preferred_element_type=jnp.float32
    )
    _, norm_back = jax.vjp(input_norm, inputs, norm_gain)
    grad_inputs, grad_norm_gain = norm_back(grad_normed)
    vector = repack(
        grad_norm_gain, grad_gate_gain, grad_kernel, grad_cbias, grad_bias, grad_rate, grad_skip
    )
    dp_count = lax.axis_size("dp")
    seq_count = lax.axis_size("seq")
    owner_rows = in_weight.shape[0]
    seq_place = lax.axis_index("seq")

    def select_rows(matrix):
        count = matrix.shape[0]
        grouped = matrix.reshape(count, dp_count, seq_count, owner_rows)
        chosen = lax.dynamic_slice_in_dim(grouped, seq_place, 1, 2)
        return chosen.reshape(count, dp_count * owner_rows)

    normed_piece = lax.all_gather(normed, "seq", axis=0, tiled=True)
    proj_piece = lax.all_gather(grad_proj, "seq", axis=0, tiled=True)
    upstream_piece = lax.all_gather(upstream, "seq", axis=0, tiled=True)
    out_piece = lax.all_gather(normed_out, "seq", axis=0, tiled=True)
    first = lax.dot_general(
        select_rows(normed_piece),
        proj_piece,
        (((0,), (0,)), ((), ())),
        preferred_element_type=jnp.float32,
    )
    second = lax.dot_general(
        select_rows(upstream_piece),
        out_piece,
        (((0,), (0,)), ((), ())),
        preferred_element_type=jnp.float32,
    )
    in_part, out_part = (
        lax.psum_scatter(
            first.reshape(dp_count, owner_rows, grad_proj.shape[1]).astype(jnp.bfloat16),
            "dp",
            scatter_dimension=0,
            tiled=True,
        ).astype(jnp.float32),
        lax.psum_scatter(
            second.reshape(dp_count, owner_rows, normed_out.shape[1]).astype(jnp.bfloat16),
            "dp",
            scatter_dimension=0,
            tiled=True,
        ).astype(jnp.float32),
    )
    in_grad = in_part.reshape(owner_rows, grad_proj.shape[1])
    out_grad = out_part.reshape(owner_rows, normed_out.shape[1])
    vec_grad = lax.psum(vector, ("dp", "seq"))
    in_new, in_m_new, in_v_new = adamw_update(in_weight, in_grad, in_m, in_v)
    out_new, out_m_new, out_v_new = adamw_update(out_weight, out_grad, out_m, out_v)
    vec_new, vec_m_new, vec_v_new = adamw_update(vec_params, vec_grad, vec_m, vec_v)
    return (
        outputs[None],
        (upstream_f + grad_inputs)[None],
        in_grad,
        out_grad,
        vec_grad,
        in_new,
        out_new,
        vec_new,
        in_m_new,
        in_v_new,
        out_m_new,
        out_v_new,
        vec_m_new,
        vec_v_new,
    )


def solution(mesh):
    in_specs = (
        P("dp", "seq", None),
        P("dp", "seq", None),
        P("dp", None),
        P(("dp", "seq"), None),
        P(("dp", "seq"), None),
        P(("dp", "seq"), None),
        P(("dp", "seq"), None),
        P(("dp", "seq"), None),
        P(("dp", "seq"), None),
        P(),
        P(),
        P(),
    )
    out_specs = (
        P("dp", "seq", None),
        P("dp", "seq", None),
        P(("dp", "seq"), None),
        P(("dp", "seq"), None),
        P(),
        P(("dp", "seq"), None),
        P(("dp", "seq"), None),
        P(),
        P(("dp", "seq"), None),
        P(("dp", "seq"), None),
        P(("dp", "seq"), None),
        P(("dp", "seq"), None),
        P(),
        P(),
    )
    return jax.shard_map(body, mesh=mesh, in_specs=in_specs, out_specs=out_specs, check_vma=False)
```

profile of v0, /device:TPU:0, one launch (start us, length us, event | category | flops | bytes accessed | tf_op | source)
XLA Modules:
  0.0 678.0 jit_solution(5091734478298455227)
XLA Ops:
  15.3 2.6 compare_convert_fusion
  17.9 76.6 %all-gather.7.cloned.1.call-done = bf16[1024,4384]{1,0:T(8,128)(2,1)} async-done(((bf16[32,4384]{1,0:T(8,128)(2,1)}), bf16[1024,4384]{1,0:T(8,128)(2,1)}) %all-gather.7.cloned.1.call-update) | async-done | bytes 8978448 | tf_op jit(solution)/shard_map/all_gather | solution.py:153
  94.5 5.1 fusion.124
  101.3 2.7 collective-permute-start.2
  115.6 2.6 copy.208
  125.2 2.7 convolution_add_fusion
  128.1 152.6 %while.7 = (s32[]{:T(128)}, f32[32,64,128]{2,1,0:T(8,128)S(1)}, f32[1,32]{1,0:T(1,128)S(1)}, f32[32,64,128]{2,1,0:T(8,128)}, s32[]{:T(128)}) while((s32[]{:T(128)}, f32[32,64,128]{2,1,0:T(8,128)S(1)}, f32[1,32]{1,0:T(1,128)S(1)}, f32[32,64,128]{2,1,0:T(8,128)}, s32[]{:T(128)}) %tuple.149), condition=%wide.region_3.4_spmd, body=%wide.region_2.3_spmd.sunk | while | flops 524290 | bytes 7340261 | solution.py:196
  128.5 2.4 multiply_add_fusion.13
  130.9 2.6 collective-permute-start
  133.5 2.4 collective-permute-done
  136.0 2.4 multiply_add_fusion.13
  138.4 23.1 %collective-permute-start = (f32[32,64,128]{2,1,0:T(8,128)}, f32[32,64,128]{2,1,0:T(8,128)S(1)}, u32[]{:S(2)}, u32[]{:S(2)}) collective-permute-start(f32[32,64,128]{2,1,0:T(8,128)} %multiply_add_fusion.13), channel_id=1, source_target_pairs={{0,1},{1,2},{2,3},{3,4},{4,5},{5,6},{6,7},{8,9},{9,10},{10,11},{11... | collective-permute-start | bytes 3145736 | tf_op jit(solution)/shard_map/while/body/eval_jaxpr/ppermute | solution.py:27
  161.5 2.4 collective-permute-done
  163.9 2.4 multiply_add_fusion.13
  166.3 27.7 %collective-permute-start = (f32[32,64,128]{2,1,0:T(8,128)}, f32[32,64,128]{2,1,0:T(8,128)S(1)}, u32[]{:S(2)}, u32[]{:S(2)}) collective-permute-start(f32[32,64,128]{2,1,0:T(8,128)} %multiply_add_fusion.13), channel_id=1, source_target_pairs={{0,1},{1,2},{2,3},{3,4},{4,5},{5,6},{6,7},{8,9},{9,10},{10,11},{11... | collective-permute-start | bytes 3145736 | tf_op jit(solution)/shard_map/while/body/eval_jaxpr/ppermute | solution.py:27
  194.0 2.4 collective-permute-done
  196.4 2.4 multiply_add_fusion.13
  198.8 22.8 %collective-permute-start = (f32[32,64,128]{2,1,0:T(8,128)}, f32[32,64,128]{2,1,0:T(8,128)S(1)}, u32[]{:S(2)}, u32[]{:S(2)}) collective-permute-start(f32[32,64,128]{2,1,0:T(8,128)} %multiply_add_fusion.13), channel_id=1, source_target_pairs={{0,1},{1,2},{2,3},{3,4},{4,5},{5,6},{6,7},{8,9},{9,10},{10,11},{11... | collective-permute-start | bytes 3145736 | tf_op jit(solution)/shard_map/while/body/eval_jaxpr/ppermute | solution.py:27
  221.6 2.4 collective-permute-done
  224.0 2.4 multiply_add_fusion.13
  226.4 14.3 %collective-permute-start = (f32[32,64,128]{2,1,0:T(8,128)}, f32[32,64,128]{2,1,0:T(8,128)S(1)}, u32[]{:S(2)}, u32[]{:S(2)}) collective-permute-start(f32[32,64,128]{2,1,0:T(8,128)} %multiply_add_fusion.13), channel_id=1, source_target_pairs={{0,1},{1,2},{2,3},{3,4},{4,5},{5,6},{6,7},{8,9},{9,10},{10,11},{11... | collective-permute-start | bytes 3145736 | tf_op jit(solution)/shard_map/while/body/eval_jaxpr/ppermute | solution.py:27
  240.8 2.4 collective-permute-done
  245.6 13.9 %collective-permute-start = (f32[32,64,128]{2,1,0:T(8,128)}, f32[32,64,128]{2,1,0:T(8,128)S(1)}, u32[]{:S(2)}, u32[]{:S(2)}) collective-permute-start(f32[32,64,128]{2,1,0:T(8,128)} %multiply_add_fusion.13), channel_id=1, source_target_pairs={{0,1},{1,2},{2,3},{3,4},{4,5},{5,6},{6,7},{8,9},{9,10},{10,11},{11... | collective-permute-start | bytes 3145736 | tf_op jit(solution)/shard_map/while/body/eval_jaxpr/ppermute | solution.py:27
  259.5 2.4 collective-permute-done
  264.3 13.9 %collective-permute-start = (f32[32,64,128]{2,1,0:T(8,128)}, f32[32,64,128]{2,1,0:T(8,128)S(1)}, u32[]{:S(2)}, u32[]{:S(2)}) collective-permute-start(f32[32,64,128]{2,1,0:T(8,128)} %multiply_add_fusion.13), channel_id=1, source_target_pairs={{0,1},{1,2},{2,3},{3,4},{4,5},{5,6},{6,7},{8,9},{9,10},{10,11},{11... | collective-permute-start | bytes 3145736 | tf_op jit(solution)/shard_map/while/body/eval_jaxpr/ppermute | solution.py:27
  278.2 2.4 collective-permute-done
  280.6 2.7 broadcast_multiply_fusion.1
  283.3 2.6 copy.205
  288.3 3.5 fusion.25
  291.8 2.5 copy.202
  294.3 3.4 multiply_reduce_fusion.13
  297.8 4.3 multiply_reduce_fusion.7
  302.2 4.2 multiply_reduce_fusion.6
  306.4 2.6 copy.207
  308.9 5.2 fusion.35
  317.0 2.9 multiply_reduce_fusion.8
  320.7 2.8 fusion.54
  323.6 134.3 %while.16 = (s32[]{:T(128)}, f32[32,64,128]{2,1,0:T(8,128)S(1)}, f32[1,32]{1,0:T(1,128)S(1)}, f32[32,64,128]{2,1,0:T(8,128)}, s32[]{:T(128)}, /*index=5*/s32[]{:T(128)}) while((s32[]{:T(128)}, f32[32,64,128]{2,1,0:T(8,128)S(1)}, f32[1,32]{1,0:T(1,128)S(1)}, f32[32,64,128]{2,1,0:T(8,128)}, s32[]{:T(128)}, ...), condition=%wide.region_8.9_spmd.clone, body=%wide.region_7.8_spmd.clone.sunk | while | flops 1310723 | bytes 6291703 | solution.py:222
  327.1 14.3 %collective-permute-done.1 = bf16[32,64,128]{2,1,0:T(8,128)(2,1)} collective-permute-done((bf16[32,64,128]{2,1,0:T(8,128)(2,1)}, bf16[32,64,128]{2,1,0:T(8,128)(2,1)}, u32[]{:S(2)}, u32[]{:S(2)}) %collective-permute-start.1) | collective-permute-done | bytes 524320 | tf_op jit(solution)/shard_map/while/body/eval_jaxpr/ppermute | solution.py:27
  346.0 10.2 %collective-permute-done.1 = bf16[32,64,128]{2,1,0:T(8,128)(2,1)} collective-permute-done((bf16[32,64,128]{2,1,0:T(8,128)(2,1)}, bf16[32,64,128]{2,1,0:T(8,128)(2,1)}, u32[]{:S(2)}, u32[]{:S(2)}) %collective-permute-start.1) | collective-permute-done | bytes 524320 | tf_op jit(solution)/shard_map/while/body/eval_jaxpr/ppermute | solution.py:27
  360.9 39.0 %collective-permute-done.1 = bf16[32,64,128]{2,1,0:T(8,128)(2,1)} collective-permute-done((bf16[32,64,128]{2,1,0:T(8,128)(2,1)}, bf16[32,64,128]{2,1,0:T(8,128)(2,1)}, u32[]{:S(2)}, u32[]{:S(2)}) %collective-permute-start.1) | collective-permute-done | bytes 524320 | tf_op jit(solution)/shard_map/while/body/eval_jaxpr/ppermute | solution.py:27
  404.5 9.5 %collective-permute-done.1 = bf16[32,64,128]{2,1,0:T(8,128)(2,1)} collective-permute-done((bf16[32,64,128]{2,1,0:T(8,128)(2,1)}, bf16[32,64,128]{2,1,0:T(8,128)(2,1)}, u32[]{:S(2)}, u32[]{:S(2)}) %collective-permute-start.1) | collective-permute-done | bytes 524320 | tf_op jit(solution)/shard_map/while/body/eval_jaxpr/ppermute | solution.py:27
  418.7 9.5 %collective-permute-done.1 = bf16[32,64,128]{2,1,0:T(8,128)(2,1)} collective-permute-done((bf16[32,64,128]{2,1,0:T(8,128)(2,1)}, bf16[32,64,128]{2,1,0:T(8,128)(2,1)}, u32[]{:S(2)}, u32[]{:S(2)}) %collective-permute-start.1) | collective-permute-done | bytes 524320 | tf_op jit(solution)/shard_map/while/body/eval_jaxpr/ppermute | solution.py:27
  432.8 9.5 %collective-permute-done.1 = bf16[32,64,128]{2,1,0:T(8,128)(2,1)} collective-permute-done((bf16[32,64,128]{2,1,0:T(8,128)(2,1)}, bf16[32,64,128]{2,1,0:T(8,128)(2,1)}, u32[]{:S(2)}, u32[]{:S(2)}) %collective-permute-start.1) | collective-permute-done | bytes 524320 | tf_op jit(solution)/shard_map/while/body/eval_jaxpr/ppermute | solution.py:27
  447.0 9.5 %collective-permute-done.1 = bf16[32,64,128]{2,1,0:T(8,128)(2,1)} collective-permute-done((bf16[32,64,128]{2,1,0:T(8,128)(2,1)}, bf16[32,64,128]{2,1,0:T(8,128)(2,1)}, u32[]{:S(2)}, u32[]{:S(2)}) %collective-permute-start.1) | collective-permute-done | bytes 524320 | tf_op jit(solution)/shard_map/while/body/eval_jaxpr/ppermute | solution.py:27
  457.9 3.3 fusion.36
  466.5 2.6 reduce_window_sum.41
  469.1 2.6 reduce_window_sum.42
  476.2 5.1 fusion.28
  481.3 2.6 copy.212
  483.9 2.5 copy.211
  486.4 3.5 fusion.120
  489.9 2.5 copy.209
  492.4 3.1 convolution_bitcast_fusion.1
  505.8 7.9 %collective-permute-done.3 = f32[3,2304]{1,0:T(4,128)S(1)} collective-permute-done((f32[3,2304]{1,0:T(4,128)S(1)}, f32[3,2304]{1,0:T(4,128)S(1)}, u32[]{:S(2)}, u32[]{:S(2)}) %collective-permute-start.3) | collective-permute-done | bytes 27680 | tf_op jit(solution)/shard_map/ppermute | solution.py:27
  514.9 2.9 copy.218
  517.9 3.9 copy.220
  522.0 3.9 fusion.9
  526.2 4.7 fusion.31
  530.9 78.9 %all-gather.13.cloned.1.call-done = bf16[1024,4384]{1,0:T(8,128)(2,1)} async-done(((bf16[128,4384]{1,0:T(8,128)(2,1)}), bf16[1024,4384]{1,0:T(8,128)(2,1)}) %all-gather.13.cloned.1.call-update) | async-done | bytes 8978448 | tf_op jit(solution)/shard_map/all_gather | solution.py:269
  609.9 6.0 fusion.4
  617.2 7.0 %multiply_reduce_fusion.14 = (f32[1024]{0:T(1024)S(1)}, f32[128]{0:T(128)S(1)}, f32[128,1024]{1,0:T(8,128)S(1)}) fusion(f32[1,128,1024]{2,1,0:T(8,128)S(1)} %copy-done.2, f32[128]{0:T(128)S(1)} %copy-done.78, f32[1024]{0:T(1024)S(1)} %slice.169, bf16[128,4384]{1,0:T(8,128)(2,1)S(1)} %copy-done.3, bf16[1024,4384]{1,0:T(8,128)(2,1)} %all-gather.7.cloned.1.call-done), kind=kOutput, calls=%fused_computation.102 | convolution fusion | flops 1150024576 | bytes 11158528 | tf_op jit(solution)/shard_map/dot_general | solution.py:249
  624.3 39.2 %psum.7 = f32[14688]{0:T(1024)S(1)} all-reduce(f32[14688]{0:T(1024)S(1)} %concatenate.23), channel_id=1, replica_groups=mesh['dp'=4,'seq'=8] {'dp','seq'}, use_global_device_ids=true, to_apply=%region_33.34 | all-reduce | flops 14688 | bytes 117504 | tf_op jit(solution)/shard_map/psum | solution.py:300
  668.5 2.4 divide_subtract_fusion
  (293 shorter events, 99.2 us)
Async XLA Ops:
  7.2 87.3 %all-gather.7.cloned.1.call-start = ((), (), s32[]{:S(2)}) async-start(), calls=%async_computation.2 | async-start | bytes 9461760 | tf_op jit(solution)/shard_map/all_gather | solution.py:153
  9.1 288.6 %all-gather.9.cloned.1.call-start = ((), (), s32[]{:S(2)}) async-start(), calls=%async_computation.3 | async-start | bytes 4325376 | tf_op jit(solution)/shard_map/all_gather | solution.py:154
  9.9 505.0 %all-gather.11.cloned.1.call-start = ((), (), s32[]{:S(2)}) async-start(), calls=%async_computation.4 | async-start | bytes 2359296 | tf_op jit(solution)/shard_map/all_gather | solution.py:268
  10.1 5.2 copy-start.81
  10.1 5.0 copy-start.77
  11.0 506.9 %all-gather.15.cloned.1.call-start = ((), (), s32[]{:S(2)}) async-start(), calls=%async_computation.6 | async-start | bytes 2359296 | tf_op jit(solution)/shard_map/all_gather | solution.py:270
  11.8 510.1 %all-gather.17.cloned.1.call-start = ((), (), s32[]{:S(2)}) async-start(), calls=%async_computation.7 | async-start | bytes 4718592 | tf_op jit(solution)/shard_map/all_gather | solution.py:271
  13.3 90.8 %copy-start.76 = (f32[32]{0:T(128)}, f32[32]{0:T(128)S(1)}, u32[]{:S(2)}) copy-start(f32[32]{0:T(128)S(1)} %get-tuple-element.499) | copy-start | bytes 388
  13.3 91.0 %copy-start.59 = (f32[32]{0:T(128)}, f32[32]{0:T(128)S(1)}, u32[]{:S(2)}) copy-start(f32[32]{0:T(128)S(1)} %get-tuple-element.498) | copy-start | bytes 388
  17.9 101.3 %copy-start.65 = (f32[128]{0:T(128)}, f32[128]{0:T(128)S(1)}, u32[]{:S(2)}) copy-start(f32[128]{0:T(128)S(1)} %get-tuple-element.509) | copy-start | bytes 1540
  99.6 16.0 %copy-start.6 = (f32[128,4384]{1,0:T(8,128)}, f32[128,4384]{1,0:T(8,128)S(1)}, u32[]{:S(2)}) copy-start(f32[128,4384]{1,0:T(8,128)S(1)} %get-tuple-element.518) | copy-start | bytes 6733828
  101.3 16.9 %collective-permute-start.2 = (bf16[3,2304]{1,0:T(4,128)(2,1)}, bf16[3,2304]{1,0:T(4,128)(2,1)}, u32[]{:S(2)}, u32[]{:S(2)}) collective-permute-start(bf16[3,2304]{1,0:T(4,128)(2,1)} %slice.205), channel_id=1, source_target_pairs={{0,1},{1,2},{2,3},{3,4},{4,5},{5,6},{6,7},{8,9},{9,10},{10,11},{11... | collective-permute-start | bytes 41480 | tf_op jit(solution)/shard_map/ppermute | solution.py:27
  108.6 212.0 %copy-start.27 = (f32[128,32]{0,1:T(8,128)}, f32[128,32]{0,1:T(8,128)S(1)}, u32[]{:S(2)}) copy-start(f32[128,32]{0,1:T(8,128)S(1)} %copy.204) | copy-start | bytes 49156
  110.8 7.4 %copy-start.47 = (f32[128,32]{0,1:T(8,128)}, f32[128,32]{0,1:T(8,128)S(1)}, u32[]{:S(2)}) copy-start(f32[128,32]{0,1:T(8,128)S(1)} %copy.201) | copy-start | bytes 49156
  130.9 5.0 collective-permute-start
  138.4 25.5 %collective-permute-start = (f32[32,64,128]{2,1,0:T(8,128)}, f32[32,64,128]{2,1,0:T(8,128)S(1)}, u32[]{:S(2)}, u32[]{:S(2)}) collective-permute-start(f32[32,64,128]{2,1,0:T(8,128)} %multiply_add_fusion.13), channel_id=1, source_target_pairs={{0,1},{1,2},{2,3},{3,4},{4,5},{5,6},{6,7},{8,9},{9,10},{10,11},{11... | collective-permute-start | bytes 3145736 | tf_op jit(solution)/shard_map/while/body/eval_jaxpr/ppermute | solution.py:27
  166.3 30.1 %collective-permute-start = (f32[32,64,128]{2,1,0:T(8,128)}, f32[32,64,128]{2,1,0:T(8,128)S(1)}, u32[]{:S(2)}, u32[]{:S(2)}) collective-permute-start(f32[32,64,128]{2,1,0:T(8,128)} %multiply_add_fusion.13), channel_id=1, source_target_pairs={{0,1},{1,2},{2,3},{3,4},{4,5},{5,6},{6,7},{8,9},{9,10},{10,11},{11... | collective-permute-start | bytes 3145736 | tf_op jit(solution)/shard_map/while/body/eval_jaxpr/ppermute | solution.py:27
  198.8 25.3 %collective-permute-start = (f32[32,64,128]{2,1,0:T(8,128)}, f32[32,64,128]{2,1,0:T(8,128)S(1)}, u32[]{:S(2)}, u32[]{:S(2)}) collective-permute-start(f32[32,64,128]{2,1,0:T(8,128)} %multiply_add_fusion.13), channel_id=1, source_target_pairs={{0,1},{1,2},{2,3},{3,4},{4,5},{5,6},{6,7},{8,9},{9,10},{10,11},{11... | collective-permute-start | bytes 3145736 | tf_op jit(solution)/shard_map/while/body/eval_jaxpr/ppermute | solution.py:27
  226.4 16.7 %collective-permute-start = (f32[32,64,128]{2,1,0:T(8,128)}, f32[32,64,128]{2,1,0:T(8,128)S(1)}, u32[]{:S(2)}, u32[]{:S(2)}) collective-permute-start(f32[32,64,128]{2,1,0:T(8,128)} %multiply_add_fusion.13), channel_id=1, source_target_pairs={{0,1},{1,2},{2,3},{3,4},{4,5},{5,6},{6,7},{8,9},{9,10},{10,11},{11... | collective-permute-start | bytes 3145736 | tf_op jit(solution)/shard_map/while/body/eval_jaxpr/ppermute | solution.py:27
  245.6 16.3 %collective-permute-start = (f32[32,64,128]{2,1,0:T(8,128)}, f32[32,64,128]{2,1,0:T(8,128)S(1)}, u32[]{:S(2)}, u32[]{:S(2)}) collective-permute-start(f32[32,64,128]{2,1,0:T(8,128)} %multiply_add_fusion.13), channel_id=1, source_target_pairs={{0,1},{1,2},{2,3},{3,4},{4,5},{5,6},{6,7},{8,9},{9,10},{10,11},{11... | collective-permute-start | bytes 3145736 | tf_op jit(solution)/shard_map/while/body/eval_jaxpr/ppermute | solution.py:27
  264.3 16.3 %collective-permute-start = (f32[32,64,128]{2,1,0:T(8,128)}, f32[32,64,128]{2,1,0:T(8,128)S(1)}, u32[]{:S(2)}, u32[]{:S(2)}) collective-permute-start(f32[32,64,128]{2,1,0:T(8,128)} %multiply_add_fusion.13), channel_id=1, source_target_pairs={{0,1},{1,2},{2,3},{3,4},{4,5},{5,6},{6,7},{8,9},{9,10},{10,11},{11... | collective-permute-start | bytes 3145736 | tf_op jit(solution)/shard_map/while/body/eval_jaxpr/ppermute | solution.py:27
  283.3 4.9 copy-start.48
  283.3 4.9 copy-start.61
  286.9 4.9 copy-start.50
  288.3 3.5 copy-start.14
  297.8 4.4 copy-start.5
  297.8 4.4 copy-start.7
  297.8 4.4 copy-start.8
  297.8 4.4 copy-start.9
  323.5 286.4 %all-gather.13.cloned.1.call-start = ((), (), s32[]{:S(2)}) async-start(), calls=%async_computation.5 | async-start | bytes 10321920 | tf_op jit(solution)/shard_map/all_gather | solution.py:269
  325.8 15.6 %collective-permute-start.1 = (bf16[32,64,128]{2,1,0:T(8,128)(2,1)}, bf16[32,64,128]{2,1,0:T(8,128)(2,1)}, u32[]{:S(2)}, u32[]{:S(2)}) collective-permute-start(bf16[32,64,128]{2,1,0:T(8,128)(2,1)} %fusion.145), channel_id=1, source_target_pairs={{1,0},{2,1},{3,2},{4,3},{5,4},{6,5},{7,6},{9,8},{10,9},{11,10},{12... | collective-permute-start | bytes 1572872 | tf_op jit(solution)/shard_map/while/body/eval_jaxpr/ppermute | solution.py:27
  344.7 11.4 %collective-permute-start.1 = (bf16[32,64,128]{2,1,0:T(8,128)(2,1)}, bf16[32,64,128]{2,1,0:T(8,128)(2,1)}, u32[]{:S(2)}, u32[]{:S(2)}) collective-permute-start(bf16[32,64,128]{2,1,0:T(8,128)(2,1)} %fusion.145), channel_id=1, source_target_pairs={{1,0},{2,1},{3,2},{4,3},{5,4},{6,5},{7,6},{9,8},{10,9},{11,10},{12... | collective-permute-start | bytes 1572872 | tf_op jit(solution)/shard_map/while/body/eval_jaxpr/ppermute | solution.py:27
  359.6 40.2 %collective-permute-start.1 = (bf16[32,64,128]{2,1,0:T(8,128)(2,1)}, bf16[32,64,128]{2,1,0:T(8,128)(2,1)}, u32[]{:S(2)}, u32[]{:S(2)}) collective-permute-start(bf16[32,64,128]{2,1,0:T(8,128)(2,1)} %fusion.145), channel_id=1, source_target_pairs={{1,0},{2,1},{3,2},{4,3},{5,4},{6,5},{7,6},{9,8},{10,9},{11,10},{12... | collective-permute-start | bytes 1572872 | tf_op jit(solution)/shard_map/while/body/eval_jaxpr/ppermute | solution.py:27
  403.2 10.8 %collective-permute-start.1 = (bf16[32,64,128]{2,1,0:T(8,128)(2,1)}, bf16[32,64,128]{2,1,0:T(8,128)(2,1)}, u32[]{:S(2)}, u32[]{:S(2)}) collective-permute-start(bf16[32,64,128]{2,1,0:T(8,128)(2,1)} %fusion.145), channel_id=1, source_target_pairs={{1,0},{2,1},{3,2},{4,3},{5,4},{6,5},{7,6},{9,8},{10,9},{11,10},{12... | collective-permute-start | bytes 1572872 | tf_op jit(solution)/shard_map/while/body/eval_jaxpr/ppermute | solution.py:27
  417.4 10.8 %collective-permute-start.1 = (bf16[32,64,128]{2,1,0:T(8,128)(2,1)}, bf16[32,64,128]{2,1,0:T(8,128)(2,1)}, u32[]{:S(2)}, u32[]{:S(2)}) collective-permute-start(bf16[32,64,128]{2,1,0:T(8,128)(2,1)} %fusion.145), channel_id=1, source_target_pairs={{1,0},{2,1},{3,2},{4,3},{5,4},{6,5},{7,6},{9,8},{10,9},{11,10},{12... | collective-permute-start | bytes 1572872 | tf_op jit(solution)/shard_map/while/body/eval_jaxpr/ppermute | solution.py:27
  431.6 10.8 %collective-permute-start.1 = (bf16[32,64,128]{2,1,0:T(8,128)(2,1)}, bf16[32,64,128]{2,1,0:T(8,128)(2,1)}, u32[]{:S(2)}, u32[]{:S(2)}) collective-permute-start(bf16[32,64,128]{2,1,0:T(8,128)(2,1)} %fusion.145), channel_id=1, source_target_pairs={{1,0},{2,1},{3,2},{4,3},{5,4},{6,5},{7,6},{9,8},{10,9},{11,10},{12... | collective-permute-start | bytes 1572872 | tf_op jit(solution)/shard_map/while/body/eval_jaxpr/ppermute | solution.py:27
  445.7 10.8 %collective-permute-start.1 = (bf16[32,64,128]{2,1,0:T(8,128)(2,1)}, bf16[32,64,128]{2,1,0:T(8,128)(2,1)}, u32[]{:S(2)}, u32[]{:S(2)}) collective-permute-start(bf16[32,64,128]{2,1,0:T(8,128)(2,1)} %fusion.145), channel_id=1, source_target_pairs={{1,0},{2,1},{3,2},{4,3},{5,4},{6,5},{7,6},{9,8},{10,9},{11,10},{12... | collective-permute-start | bytes 1572872 | tf_op jit(solution)/shard_map/while/body/eval_jaxpr/ppermute | solution.py:27
  489.9 5.7 copy-start.28
  497.4 4.1 copy-start.10
  497.5 4.1 copy-start.13
  497.5 4.1 copy-start.66
  497.5 4.1 copy-start.68
  497.5 4.1 copy-start.70
  503.9 9.8 %collective-permute-start.3 = (f32[3,2304]{1,0:T(4,128)S(1)}, f32[3,2304]{1,0:T(4,128)S(1)}, u32[]{:S(2)}, u32[]{:S(2)}) collective-permute-start(f32[3,2304]{1,0:T(4,128)S(1)} %pad_add_fusion.1), channel_id=1, source_target_pairs={{1,0},{2,1},{3,2},{4,3},{5,4},{6,5},{7,6},{9,8},{10,9},{11,10},{12... | collective-permute-start | bytes 82952 | tf_op jit(solution)/shard_map/ppermute | solution.py:27
  505.7 8.0 %copy-start.19 = (bf16[128,2048]{1,0:T(8,128)(2,1)S(1)}, bf16[128,2048]{1,0:T(8,128)(2,1)}, u32[]{:S(2)}) copy-start(bf16[128,2048]{1,0:T(8,128)(2,1)} %get-tuple-element.479) | copy-start | bytes 1572868
  505.8 8.0 %copy-start.37 = (bf16[128,32]{1,0:T(8,128)(2,1)S(1)}, bf16[128,32]{1,0:T(8,128)(2,1)}, u32[]{:S(2)}) copy-start(bf16[128,32]{1,0:T(8,128)(2,1)} %get-tuple-element.473) | copy-start | bytes 24580
  514.9 151.3 %reduce-scatter.9.cloned.1.call-start = ((), (), s32[]{:S(2)}) async-start(), calls=%async_computation.9 | async-start | bytes 655360
  517.8 4.0 copy-start.54
  517.8 4.0 copy-start.53
  517.8 4.0 copy-start.52
  521.9 4.1 copy-start.57
  521.9 4.2 copy-start.2
  522.0 4.2 copy-start.12
  525.9 142.6 %reduce-scatter.7.cloned.1.call-start = ((), (), s32[]{:S(2)}) async-start(), calls=%async_computation.8 | async-start | bytes 1433600
  609.9 6.1 copy-start.83
  609.9 6.2 copy-start.78
  617.2 7.0 %copy-start.55 = (f32[2304]{0:T(1024)S(1)}, f32[2304]{0:T(1024)}, u32[]{:S(2)}) copy-start(f32[2304]{0:T(1024)} %get-tuple-element.436) | copy-start | bytes 27652
  617.2 7.0 %copy-start.58 = (f32[2048]{0:T(1024)S(1)}, f32[2048]{0:T(1024)}, u32[]{:S(2)}) copy-start(f32[2048]{0:T(1024)} %get-tuple-element.434) | copy-start | bytes 24580
  617.2 7.0 %copy-start.80 = (f32[32]{0:T(128)S(1)}, f32[32]{0:T(128)}, u32[]{:S(2)}) copy-start(f32[32]{0:T(128)} %get-tuple-element.472) | copy-start | bytes 388
  617.2 46.3 %copy-start.82 = (f32[128]{0:T(128)S(1)}, f32[128]{0:T(128)}, u32[]{:S(2)}) copy-start(f32[128]{0:T(128)} %copy-done.81) | copy-start | bytes 1540
  617.2 46.3 %copy-start.21 = (f32[1,128,1024]{2,1,0:T(8,128)S(1)}, f32[1,128,1024]{2,1,0:T(8,128)}, u32[]{:S(2)}) copy-start(f32[1,128,1024]{2,1,0:T(8,128)} %param.17) | copy-start | bytes 1572868
  664.5 4.0 copy-start.18
  664.5 4.0 copy-start.24
  664.5 4.0 copy-start.25
  (44 other events, 83.5 us)
Sparse Core Ops, SparseCore 0:
  11.4 82.9 all-gather.6
  98.1 60.2 all-gather.8
  160.5 32.0 all-gather.10
  194.6 31.4 all-gather.14
  323.6 73.2 all-gather.16
  515.0 94.8 all-gather.12
  613.3 23.5 reduce-scatter.8
  639.7 28.6 reduce-scatter.6
where the time goes:
time: 686 us; the launch traced here: 678 us
  waiting for transfers between devices  282 us (41%)
  starting transfers between devices  132 us (19%)
  other arithmetic  89.3 us (13%)
  matrix products  67.5 us (10%)
  local copies, waits for them, and re-layouts  51.8 us (8%)
  blocking collectives  39.2 us (6%)
  between operations  15.4 us (2%)
    ppermute x16, starting transfers between devices, shifted_2(): return lax.ppermute(block, axis, route)  131 us
    ppermute x16, waiting for transfers between devices, shifted_2(): return lax.ppermute(block, axis, route)  126 us
    all_gather x1, waiting for transfers between devices, body(): proj_piece = lax.all_gather(grad_proj, 'seq', axis=0, tiled=True)  78.9 us
    all_gather x1, waiting for transfers between devices, body(): lax.all_gather(in_weight.astype(jnp.bfloat16), ('dp', 'seq'), axis=0, til...  76.6 us
    psum x1, blocking collectives, body(): vec_grad = lax.psum(vector, ('dp', 'seq'))  39.2 us
    add x7, other arithmetic, relay(): return shifted_2(decay[:, None, None] * entry_now + local_state, 'seq', 1)  16.8 us
    convert_element_type x7, other arithmetic, back_relay(): (own_part + decay[:, None, None] * later).astype(jnp.bfloat16)  15.5 us
    dot_general x3, matrix products, ssd_block(): inside = jnp.einsum('hij,jhp->ihp', mixing, values, precision=top_precision)  13.7 us
  transfers between devices with their start and end apart: 24, of which 18 were waited for; matrix products, arithmetic and copies ran while one was open for 30% of the time, Pallas kernels for 0%

commit v1 on v0

--- a/solution.py
+++ b/solution.py
@@ -19,6 +19,27 @@
 decay_rate = 0.1
 adam_eps = 1e-08
 top_precision = lax.Precision.HIGHEST
+
+
+def collect(array, axis, dim):
+    size, place, rows = (lax.axis_size(axis), lax.axis_index(axis), array.shape[dim])
+    ahead = [(i, (i + 1) % size) for i in range(size)]
+    left = [(i, (i - 1) % size) for i in range(size)]
+    out = jnp.zeros((*array.shape[:dim], size * rows, *array.shape[dim + 1 :]), array.dtype)
+    out = lax.dynamic_update_slice_in_dim(out, array, place * rows, axis=dim)
+    from_left = from_right = array
+    half = size // 2
+    for step in range(1, half + 1):
+        from_left = lax.ppermute(from_left, axis, ahead)
+        out = lax.dynamic_update_slice_in_dim(
+            out, from_left, (place - step) % size * rows, axis=dim
+        )
+        if step < size - half:
+            from_right = lax.ppermute(from_right, axis, left)
+            out = lax.dynamic_update_slice_in_dim(
+                out, from_right, (place + step) % size * rows, axis=dim
+            )
+    return out
 
 
 def shifted_2(block, axis, distance):
@@ -266,7 +287,7 @@
         return chosen.reshape(count, dp_count * owner_rows)
 
     normed_piece = lax.all_gather(normed, "seq", axis=0, tiled=True)
-    proj_piece = lax.all_gather(grad_proj, "seq", axis=0, tiled=True)
+    proj_piece = collect(grad_proj, "seq", 0)
     upstream_piece = lax.all_gather(upstream, "seq", axis=0, tiled=True)
     out_piece = lax.all_gather(normed_out, "seq", axis=0, tiled=True)
     first = lax.dot_general(

time: 686 us -> 729 us (1.063)
  starting transfers between devices: 132 us -> 166 us
  blocking collectives: 39.2 us -> 47.5 us
  local copies, waits for them, and re-layouts: 51.8 us -> 59.7 us
    ppermute x0 -> x7, waiting for transfers between devices: none -> 79.4 us  [the longest x4 68.3 us: collect(): from_left = lax.ppermute(from_left, axis, ahead)]
    all_gather x1 -> x0, waiting for transfers between devices: 78.9 us -> none  [body(): proj_piece = lax.all_gather(grad_proj, 'seq', axis=0, tiled=True)]
    ppermute x16, waiting for transfers between devices: 126 us -> 95.8 us  [shifted_2(): return lax.ppermute(block, axis, route)]
    ppermute x0 -> x7, starting transfers between devices: none -> 25.2 us  [the longest x4 15.9 us: collect(): from_left = lax.ppermute(from_left, axis, ahead)]
    unnamed x10 -> x9, waiting for transfers between devices: 0.41 us -> 23.1 us
    ppermute x16, starting transfers between devices: 131 us -> 140 us  [shifted_2(): return lax.ppermute(block, axis, route)]
    psum x1, blocking collectives: 39.2 us -> 47.5 us  [body(): vec_grad = lax.psum(vector, ('dp', 'seq'))]
  transfers between devices with their start and end apart: 24 -> 30, of which waited for: 18 -> 24; matrix products, arithmetic and copies ran while one was open for 30% -> 29% of each run, Pallas kernels for 0% -> 0%
where the time goes in v1:
time: 729 us; the launch traced here: 721 us
  waiting for transfers between devices  275 us (38%)
  starting transfers between devices  166 us (23%)
  other arithmetic  91.2 us (13%)
  matrix products  65.1 us (9%)
  local copies, waits for them, and re-layouts  59.7 us (8%)
  blocking collectives  47.5 us (7%)
  between operations  15.5 us (2%)
    ppermute x16, starting transfers between devices, shifted_2(): return lax.ppermute(block, axis, route)  140 us
    ppermute x16, waiting for transfers between devices, shifted_2(): return lax.ppermute(block, axis, route)  95.8 us
    all_gather x1, waiting for transfers between devices, body(): lax.all_gather(in_weight.astype(jnp.bfloat16), ('dp', 'seq'), axis=0, til...  77.1 us
    ppermute x4, waiting for transfers between devices, collect(): from_left = lax.ppermute(from_left, axis, ahead)  68.3 us
    psum x1, blocking collectives, body(): vec_grad = lax.psum(vector, ('dp', 'seq'))  47.5 us
    unnamed x9, waiting for transfers between devices  23.1 us
    add x7, other arithmetic, relay(): return shifted_2(decay[:, None, None] * entry_now + local_state, 'seq', 1)  17.6 us
    ppermute x4, starting transfers between devices, collect(): from_left = lax.ppermute(from_left, axis, ahead)  15.9 us
  transfers between devices with their start and end apart: 30, of which 24 were waited for; matrix products, arithmetic and copies ran while one was open for 29% of the time, Pallas kernels for 0%

profile of v1, /device:TPU:0, one launch (start us, length us, event | category | flops | bytes accessed | tf_op | source)
XLA Modules:
  0.0 721.1 jit_solution(7520746127508885010)
XLA Ops:
  14.7 2.6 compare_convert_fusion
  17.3 77.1 %all-gather.6.cloned.1.call-done = bf16[1024,4384]{1,0:T(8,128)(2,1)} async-done(((bf16[32,4384]{1,0:T(8,128)(2,1)}), bf16[1024,4384]{1,0:T(8,128)(2,1)}) %all-gather.6.cloned.1.call-update) | async-done | bytes 8978448 | tf_op jit(solution)/shard_map/all_gather | solution.py:174
  94.5 5.1 fusion.124
  101.3 2.7 collective-permute-start.2
  117.1 2.6 copy.222
  130.9 162.2 %while.7 = (s32[]{:T(128)}, f32[32,64,128]{2,1,0:T(8,128)S(1)}, f32[1,32]{1,0:T(1,128)S(1)}, f32[32,64,128]{2,1,0:T(8,128)}, s32[]{:T(128)}) while((s32[]{:T(128)}, f32[32,64,128]{2,1,0:T(8,128)S(1)}, f32[1,32]{1,0:T(1,128)S(1)}, f32[32,64,128]{2,1,0:T(8,128)}, s32[]{:T(128)}) %tuple.147), condition=%wide.region_3.4_spmd, body=%wide.region_2.3_spmd.sunk | while | flops 524290 | bytes 7340261 | solution.py:217
  134.0 2.6 collective-permute-start
  139.0 2.8 multiply_add_fusion.13
  141.8 22.8 %collective-permute-start = (f32[32,64,128]{2,1,0:T(8,128)}, f32[32,64,128]{2,1,0:T(8,128)S(1)}, u32[]{:S(2)}, u32[]{:S(2)}) collective-permute-start(f32[32,64,128]{2,1,0:T(8,128)} %multiply_add_fusion.13), channel_id=1, source_target_pairs={{0,1},{1,2},{2,3},{3,4},{4,5},{5,6},{6,7},{8,9},{9,10},{10,11},{11... | collective-permute-start | bytes 3145736 | tf_op jit(solution)/shard_map/while/body/eval_jaxpr/ppermute | solution.py:48
  167.0 2.5 multiply_add_fusion.13
  169.5 30.7 %collective-permute-start = (f32[32,64,128]{2,1,0:T(8,128)}, f32[32,64,128]{2,1,0:T(8,128)S(1)}, u32[]{:S(2)}, u32[]{:S(2)}) collective-permute-start(f32[32,64,128]{2,1,0:T(8,128)} %multiply_add_fusion.13), channel_id=1, source_target_pairs={{0,1},{1,2},{2,3},{3,4},{4,5},{5,6},{6,7},{8,9},{9,10},{10,11},{11... | collective-permute-start | bytes 3145736 | tf_op jit(solution)/shard_map/while/body/eval_jaxpr/ppermute | solution.py:48
  205.1 29.2 %collective-permute-start = (f32[32,64,128]{2,1,0:T(8,128)}, f32[32,64,128]{2,1,0:T(8,128)S(1)}, u32[]{:S(2)}, u32[]{:S(2)}) collective-permute-start(f32[32,64,128]{2,1,0:T(8,128)} %multiply_add_fusion.13), channel_id=1, source_target_pairs={{0,1},{1,2},{2,3},{3,4},{4,5},{5,6},{6,7},{8,9},{9,10},{10,11},{11... | collective-permute-start | bytes 3145736 | tf_op jit(solution)/shard_map/while/body/eval_jaxpr/ppermute | solution.py:48
  239.2 13.9 %collective-permute-start = (f32[32,64,128]{2,1,0:T(8,128)}, f32[32,64,128]{2,1,0:T(8,128)S(1)}, u32[]{:S(2)}, u32[]{:S(2)}) collective-permute-start(f32[32,64,128]{2,1,0:T(8,128)} %multiply_add_fusion.13), channel_id=1, source_target_pairs={{0,1},{1,2},{2,3},{3,4},{4,5},{5,6},{6,7},{8,9},{9,10},{10,11},{11... | collective-permute-start | bytes 3145736 | tf_op jit(solution)/shard_map/while/body/eval_jaxpr/ppermute | solution.py:48
  258.0 13.9 %collective-permute-start = (f32[32,64,128]{2,1,0:T(8,128)}, f32[32,64,128]{2,1,0:T(8,128)S(1)}, u32[]{:S(2)}, u32[]{:S(2)}) collective-permute-start(f32[32,64,128]{2,1,0:T(8,128)} %multiply_add_fusion.13), channel_id=1, source_target_pairs={{0,1},{1,2},{2,3},{3,4},{4,5},{5,6},{6,7},{8,9},{9,10},{10,11},{11... | collective-permute-start | bytes 3145736 | tf_op jit(solution)/shard_map/while/body/eval_jaxpr/ppermute | solution.py:48
  276.8 13.9 %collective-permute-start = (f32[32,64,128]{2,1,0:T(8,128)}, f32[32,64,128]{2,1,0:T(8,128)S(1)}, u32[]{:S(2)}, u32[]{:S(2)}) collective-permute-start(f32[32,64,128]{2,1,0:T(8,128)} %multiply_add_fusion.13), channel_id=1, source_target_pairs={{0,1},{1,2},{2,3},{3,4},{4,5},{5,6},{6,7},{8,9},{9,10},{10,11},{11... | collective-permute-start | bytes 3145736 | tf_op jit(solution)/shard_map/while/body/eval_jaxpr/ppermute | solution.py:48
  293.1 2.7 broadcast_multiply_fusion.1
  295.8 2.7 copy.219
  298.5 4.9 fusion.25
  303.4 2.6 copy.216
  306.0 3.4 multiply_reduce_fusion.13
  309.5 4.3 multiply_reduce_fusion.7
  313.8 4.1 multiply_reduce_fusion.6
  317.9 2.6 copy.221
  320.5 2.8 fusion.54
  323.4 104.7 %while.16 = (s32[]{:T(128)}, f32[32,64,128]{2,1,0:T(8,128)S(1)}, f32[1,32]{1,0:T(1,128)S(1)}, f32[32,64,128]{2,1,0:T(8,128)}, s32[]{:T(128)}, /*index=5*/s32[]{:T(128)}) while((s32[]{:T(128)}, f32[32,64,128]{2,1,0:T(8,128)S(1)}, f32[1,32]{1,0:T(1,128)S(1)}, f32[32,64,128]{2,1,0:T(8,128)}, s32[]{:T(128)}, ...), condition=%wide.region_8.9_spmd.clone, body=%wide.region_7.8_spmd.clone.sunk | while | flops 1310723 | bytes 6291703 | solution.py:243
  326.9 14.3 %collective-permute-done.1 = bf16[32,64,128]{2,1,0:T(8,128)(2,1)} collective-permute-done((bf16[32,64,128]{2,1,0:T(8,128)(2,1)}, bf16[32,64,128]{2,1,0:T(8,128)(2,1)}, u32[]{:S(2)}, u32[]{:S(2)}) %collective-permute-start.1) | collective-permute-done | bytes 524320 | tf_op jit(solution)/shard_map/while/body/eval_jaxpr/ppermute | solution.py:48
  345.9 10.2 %collective-permute-done.1 = bf16[32,64,128]{2,1,0:T(8,128)(2,1)} collective-permute-done((bf16[32,64,128]{2,1,0:T(8,128)(2,1)}, bf16[32,64,128]{2,1,0:T(8,128)(2,1)}, u32[]{:S(2)}, u32[]{:S(2)}) %collective-permute-start.1) | collective-permute-done | bytes 524320 | tf_op jit(solution)/shard_map/while/body/eval_jaxpr/ppermute | solution.py:48
  360.7 9.5 %collective-permute-done.1 = bf16[32,64,128]{2,1,0:T(8,128)(2,1)} collective-permute-done((bf16[32,64,128]{2,1,0:T(8,128)(2,1)}, bf16[32,64,128]{2,1,0:T(8,128)(2,1)}, u32[]{:S(2)}, u32[]{:S(2)}) %collective-permute-start.1) | collective-permute-done | bytes 524320 | tf_op jit(solution)/shard_map/while/body/eval_jaxpr/ppermute | solution.py:48
  374.9 9.5 %collective-permute-done.1 = bf16[32,64,128]{2,1,0:T(8,128)(2,1)} collective-permute-done((bf16[32,64,128]{2,1,0:T(8,128)(2,1)}, bf16[32,64,128]{2,1,0:T(8,128)(2,1)}, u32[]{:S(2)}, u32[]{:S(2)}) %collective-permute-start.1) | collective-permute-done | bytes 524320 | tf_op jit(solution)/shard_map/while/body/eval_jaxpr/ppermute | solution.py:48
  389.1 9.5 %collective-permute-done.1 = bf16[32,64,128]{2,1,0:T(8,128)(2,1)} collective-permute-done((bf16[32,64,128]{2,1,0:T(8,128)(2,1)}, bf16[32,64,128]{2,1,0:T(8,128)(2,1)}, u32[]{:S(2)}, u32[]{:S(2)}) %collective-permute-start.1) | collective-permute-done | bytes 524320 | tf_op jit(solution)/shard_map/while/body/eval_jaxpr/ppermute | solution.py:48
  403.3 9.5 %collective-permute-done.1 = bf16[32,64,128]{2,1,0:T(8,128)(2,1)} collective-permute-done((bf16[32,64,128]{2,1,0:T(8,128)(2,1)}, bf16[32,64,128]{2,1,0:T(8,128)(2,1)}, u32[]{:S(2)}, u32[]{:S(2)}) %collective-permute-start.1) | collective-permute-done | bytes 524320 | tf_op jit(solution)/shard_map/while/body/eval_jaxpr/ppermute | solution.py:48
  417.4 9.5 %collective-permute-done.1 = bf16[32,64,128]{2,1,0:T(8,128)(2,1)} collective-permute-done((bf16[32,64,128]{2,1,0:T(8,128)(2,1)}, bf16[32,64,128]{2,1,0:T(8,128)(2,1)}, u32[]{:S(2)}, u32[]{:S(2)}) %collective-permute-start.1) | collective-permute-done | bytes 524320 | tf_op jit(solution)/shard_map/while/body/eval_jaxpr/ppermute | solution.py:48
  429.2 2.5 fusion.36
  431.7 4.4 fusion.35
  445.6 2.6 reduce_window_sum.41
  448.1 2.6 reduce_window_sum.42
  455.3 5.1 fusion.28
  460.3 2.6 copy.226
  462.9 2.5 copy.225
  465.4 3.6 fusion.120
  469.0 2.5 copy.223
  471.5 3.1 convolution_bitcast_fusion.1
  487.2 6.9 collective-permute-done.3
  496.1 2.7 collective-permute-start.4
  500.6 4.0 copy.232
  504.7 4.1 copy.236
  508.8 4.5 fusion.31
  514.9 24.6 %collective-permute-done.4 = bf16[128,4384]{0,1:T(8,128)(2,1)} collective-permute-done((bf16[128,4384]{0,1:T(8,128)(2,1)S(1)}, bf16[128,4384]{0,1:T(8,128)(2,1)}, u32[]{:S(2)}, u32[]{:S(2)}) %collective-permute-start.4) | collective-permute-done | bytes 1122336 | tf_op jit(solution)/shard_map/ppermute | solution.py:33
  539.5 4.4 collective-permute-start.6
  544.0 4.6 collective-permute-done.5
  548.6 3.8 collective-permute-start.7
  555.7 19.9 %collective-permute-done.6 = bf16[128,4384]{0,1:T(8,128)(2,1)S(1)} collective-permute-done((bf16[128,4384]{0,1:T(8,128)(2,1)}, bf16[128,4384]{0,1:T(8,128)(2,1)S(1)}, u32[]{:S(2)}, u32[]{:S(2)}) %collective-permute-start.6) | collective-permute-done | bytes 1122336 | tf_op jit(solution)/shard_map/ppermute | solution.py:33
  575.6 4.6 collective-permute-start.8
  582.1 3.7 collective-permute-start.9
  586.6 12.4 %collective-permute-done.8 = bf16[128,4384]{0,1:T(8,128)(2,1)S(1)} collective-permute-done((bf16[128,4384]{0,1:T(8,128)(2,1)S(1)}, bf16[128,4384]{0,1:T(8,128)(2,1)S(1)}, u32[]{:S(2)}, u32[]{:S(2)}) %collective-permute-start.8) | collective-permute-done | bytes 1122336 | tf_op jit(solution)/shard_map/ppermute | solution.py:33
  599.0 4.1 collective-permute-start.10
  603.5 4.5 collective-permute-done.9
  608.4 11.4 %collective-permute-done.10 = bf16[128,4384]{0,1:T(8,128)(2,1)S(1)} collective-permute-done((bf16[128,4384]{0,1:T(8,128)(2,1)S(1)}, bf16[128,4384]{0,1:T(8,128)(2,1)S(1)}, u32[]{:S(2)}, u32[]{:S(2)}) %collective-permute-start.10) | collective-permute-done | bytes 1122336 | tf_op jit(solution)/shard_map/ppermute | solution.py:33
  620.2 5.0 fusion.4
  626.3 6.8 multiply_reduce_fusion.14
  633.2 47.5 %psum.7 = f32[14688]{0:T(1024)S(1)} all-reduce(f32[14688]{0:T(1024)S(1)} %concatenate.23), channel_id=1, replica_groups=mesh['dp'=4,'seq'=8] {'dp','seq'}, use_global_device_ids=true, to_apply=%region_33.34 | all-reduce | flops 14688 | bytes 117504 | tf_op jit(solution)/shard_map/psum | solution.py:321
  682.5 3.9 fusion.9
  686.6 2.5 divide_subtract_fusion
  689.1 23.0 %reduce-scatter.9.cloned.1.call-done = bf16[1,32,2048]{2,1,0:T(8,128)(2,1)} async-done(((bf16[4,32,2048]{2,1,0:T(8,128)(2,1)}), bf16[1,32,2048]{2,1,0:T(8,128)(2,1)}) %reduce-scatter.9.cloned.1.call-update) | async-done | bytes 131088
  (304 shorter events, 139.6 us)
Async XLA Ops:
  7.2 87.3 %all-gather.6.cloned.1.call-start = ((), (), s32[]{:S(2)}) async-start(), calls=%async_computation.2 | async-start | bytes 9461760 | tf_op jit(solution)/shard_map/all_gather | solution.py:174
  9.1 300.3 %all-gather.8.cloned.1.call-start = ((), (), s32[]{:S(2)}) async-start(), calls=%async_computation.3 | async-start | bytes 4325376 | tf_op jit(solution)/shard_map/all_gather | solution.py:175
  9.9 490.7 %all-gather.10.cloned.1.call-start = ((), (), s32[]{:S(2)}) async-start(), calls=%async_computation.4 | async-start | bytes 2359296 | tf_op jit(solution)/shard_map/all_gather | solution.py:289
  11.0 493.7 %all-gather.12.cloned.1.call-start = ((), (), s32[]{:S(2)}) async-start(), calls=%async_computation.5 | async-start | bytes 2359296 | tf_op jit(solution)/shard_map/all_gather | solution.py:291
  11.8 670.7 %all-gather.14.cloned.1.call-start = ((), (), s32[]{:S(2)}) async-start(), calls=%async_computation.6 | async-start | bytes 4718592 | tf_op jit(solution)/shard_map/all_gather | solution.py:292
  12.5 108.3 %copy-start.36 = (f32[2304]{0:T(1024)}, f32[2304]{0:T(1024)S(1)}, u32[]{:S(2)}) copy-start(f32[2304]{0:T(1024)S(1)} %get-tuple-element.502) | copy-start | bytes 27652
  12.5 108.3 %copy-start.38 = (f32[2304]{0:T(1024)}, f32[2304]{0:T(1024)S(1)}, u32[]{:S(2)}) copy-start(f32[2304]{0:T(1024)S(1)} %get-tuple-element.503) | copy-start | bytes 27652
  13.3 90.8 %copy-start.70 = (f32[32]{0:T(128)}, f32[32]{0:T(128)S(1)}, u32[]{:S(2)}) copy-start(f32[32]{0:T(128)S(1)} %get-tuple-element.499) | copy-start | bytes 388
  13.3 91.0 %copy-start.56 = (f32[32]{0:T(128)}, f32[32]{0:T(128)S(1)}, u32[]{:S(2)}) copy-start(f32[32]{0:T(128)S(1)} %get-tuple-element.498) | copy-start | bytes 388
  17.3 87.0 %copy-start.68 = (f32[128]{0:T(128)}, f32[128]{0:T(128)S(1)}, u32[]{:S(2)}) copy-start(f32[128]{0:T(128)S(1)} %get-tuple-element.506) | copy-start | bytes 1540
  17.3 87.0 %copy-start.69 = (f32[128]{0:T(128)}, f32[128]{0:T(128)S(1)}, u32[]{:S(2)}) copy-start(f32[128]{0:T(128)S(1)} %get-tuple-element.507) | copy-start | bytes 1540
  17.3 103.4 %copy-start.61 = (f32[128]{0:T(128)}, f32[128]{0:T(128)S(1)}, u32[]{:S(2)}) copy-start(f32[128]{0:T(128)S(1)} %get-tuple-element.509) | copy-start | bytes 1540
  99.6 17.5 %copy-start.8 = (f32[128,4384]{1,0:T(8,128)}, f32[128,4384]{1,0:T(8,128)S(1)}, u32[]{:S(2)}) copy-start(f32[128,4384]{1,0:T(8,128)S(1)} %get-tuple-element.518) | copy-start | bytes 6733828
  101.3 18.4 %collective-permute-start.2 = (bf16[3,2304]{1,0:T(4,128)(2,1)}, bf16[3,2304]{1,0:T(4,128)(2,1)}, u32[]{:S(2)}, u32[]{:S(2)}) collective-permute-start(bf16[3,2304]{1,0:T(4,128)(2,1)} %slice.205), channel_id=1, source_target_pairs={{0,1},{1,2},{2,3},{3,4},{4,5},{5,6},{6,7},{8,9},{9,10},{10,11},{11... | collective-permute-start | bytes 41480 | tf_op jit(solution)/shard_map/ppermute | solution.py:48
  104.3 4.5 copy-start.67
  123.3 5.0 copy-start.6
  124.6 4.5 copy-start.43
  124.6 4.5 copy-start.77
  134.0 5.0 collective-permute-start
  141.8 25.2 %collective-permute-start = (f32[32,64,128]{2,1,0:T(8,128)}, f32[32,64,128]{2,1,0:T(8,128)S(1)}, u32[]{:S(2)}, u32[]{:S(2)}) collective-permute-start(f32[32,64,128]{2,1,0:T(8,128)} %multiply_add_fusion.13), channel_id=1, source_target_pairs={{0,1},{1,2},{2,3},{3,4},{4,5},{5,6},{6,7},{8,9},{9,10},{10,11},{11... | collective-permute-start | bytes 3145736 | tf_op jit(solution)/shard_map/while/body/eval_jaxpr/ppermute | solution.py:48
  169.5 33.1 %collective-permute-start = (f32[32,64,128]{2,1,0:T(8,128)}, f32[32,64,128]{2,1,0:T(8,128)S(1)}, u32[]{:S(2)}, u32[]{:S(2)}) collective-permute-start(f32[32,64,128]{2,1,0:T(8,128)} %multiply_add_fusion.13), channel_id=1, source_target_pairs={{0,1},{1,2},{2,3},{3,4},{4,5},{5,6},{6,7},{8,9},{9,10},{10,11},{11... | collective-permute-start | bytes 3145736 | tf_op jit(solution)/shard_map/while/body/eval_jaxpr/ppermute | solution.py:48
  205.1 31.6 %collective-permute-start = (f32[32,64,128]{2,1,0:T(8,128)}, f32[32,64,128]{2,1,0:T(8,128)S(1)}, u32[]{:S(2)}, u32[]{:S(2)}) collective-permute-start(f32[32,64,128]{2,1,0:T(8,128)} %multiply_add_fusion.13), channel_id=1, source_target_pairs={{0,1},{1,2},{2,3},{3,4},{4,5},{5,6},{6,7},{8,9},{9,10},{10,11},{11... | collective-permute-start | bytes 3145736 | tf_op jit(solution)/shard_map/while/body/eval_jaxpr/ppermute | solution.py:48
  239.2 16.3 %collective-permute-start = (f32[32,64,128]{2,1,0:T(8,128)}, f32[32,64,128]{2,1,0:T(8,128)S(1)}, u32[]{:S(2)}, u32[]{:S(2)}) collective-permute-start(f32[32,64,128]{2,1,0:T(8,128)} %multiply_add_fusion.13), channel_id=1, source_target_pairs={{0,1},{1,2},{2,3},{3,4},{4,5},{5,6},{6,7},{8,9},{9,10},{10,11},{11... | collective-permute-start | bytes 3145736 | tf_op jit(solution)/shard_map/while/body/eval_jaxpr/ppermute | solution.py:48
  258.0 16.3 %collective-permute-start = (f32[32,64,128]{2,1,0:T(8,128)}, f32[32,64,128]{2,1,0:T(8,128)S(1)}, u32[]{:S(2)}, u32[]{:S(2)}) collective-permute-start(f32[32,64,128]{2,1,0:T(8,128)} %multiply_add_fusion.13), channel_id=1, source_target_pairs={{0,1},{1,2},{2,3},{3,4},{4,5},{5,6},{6,7},{8,9},{9,10},{10,11},{11... | collective-permute-start | bytes 3145736 | tf_op jit(solution)/shard_map/while/body/eval_jaxpr/ppermute | solution.py:48
  276.8 16.3 %collective-permute-start = (f32[32,64,128]{2,1,0:T(8,128)}, f32[32,64,128]{2,1,0:T(8,128)S(1)}, u32[]{:S(2)}, u32[]{:S(2)}) collective-permute-start(f32[32,64,128]{2,1,0:T(8,128)} %multiply_add_fusion.13), channel_id=1, source_target_pairs={{0,1},{1,2},{2,3},{3,4},{4,5},{5,6},{6,7},{8,9},{9,10},{10,11},{11... | collective-permute-start | bytes 3145736 | tf_op jit(solution)/shard_map/while/body/eval_jaxpr/ppermute | solution.py:48
  309.4 4.4 copy-start.7
  309.4 4.4 copy-start.9
  309.4 4.4 copy-start.10
  309.5 4.4 copy-start.11
  325.6 15.6 %collective-permute-start.1 = (bf16[32,64,128]{2,1,0:T(8,128)(2,1)}, bf16[32,64,128]{2,1,0:T(8,128)(2,1)}, u32[]{:S(2)}, u32[]{:S(2)}) collective-permute-start(bf16[32,64,128]{2,1,0:T(8,128)(2,1)} %fusion.145), channel_id=1, source_target_pairs={{1,0},{2,1},{3,2},{4,3},{5,4},{6,5},{7,6},{9,8},{10,9},{11,10},{12... | collective-permute-start | bytes 1572872 | tf_op jit(solution)/shard_map/while/body/eval_jaxpr/ppermute | solution.py:48
  344.6 11.4 %collective-permute-start.1 = (bf16[32,64,128]{2,1,0:T(8,128)(2,1)}, bf16[32,64,128]{2,1,0:T(8,128)(2,1)}, u32[]{:S(2)}, u32[]{:S(2)}) collective-permute-start(bf16[32,64,128]{2,1,0:T(8,128)(2,1)} %fusion.145), channel_id=1, source_target_pairs={{1,0},{2,1},{3,2},{4,3},{5,4},{6,5},{7,6},{9,8},{10,9},{11,10},{12... | collective-permute-start | bytes 1572872 | tf_op jit(solution)/shard_map/while/body/eval_jaxpr/ppermute | solution.py:48
  359.4 10.8 %collective-permute-start.1 = (bf16[32,64,128]{2,1,0:T(8,128)(2,1)}, bf16[32,64,128]{2,1,0:T(8,128)(2,1)}, u32[]{:S(2)}, u32[]{:S(2)}) collective-permute-start(bf16[32,64,128]{2,1,0:T(8,128)(2,1)} %fusion.145), channel_id=1, source_target_pairs={{1,0},{2,1},{3,2},{4,3},{5,4},{6,5},{7,6},{9,8},{10,9},{11,10},{12... | collective-permute-start | bytes 1572872 | tf_op jit(solution)/shard_map/while/body/eval_jaxpr/ppermute | solution.py:48
  373.6 10.8 %collective-permute-start.1 = (bf16[32,64,128]{2,1,0:T(8,128)(2,1)}, bf16[32,64,128]{2,1,0:T(8,128)(2,1)}, u32[]{:S(2)}, u32[]{:S(2)}) collective-permute-start(bf16[32,64,128]{2,1,0:T(8,128)(2,1)} %fusion.145), channel_id=1, source_target_pairs={{1,0},{2,1},{3,2},{4,3},{5,4},{6,5},{7,6},{9,8},{10,9},{11,10},{12... | collective-permute-start | bytes 1572872 | tf_op jit(solution)/shard_map/while/body/eval_jaxpr/ppermute | solution.py:48
  387.8 10.8 %collective-permute-start.1 = (bf16[32,64,128]{2,1,0:T(8,128)(2,1)}, bf16[32,64,128]{2,1,0:T(8,128)(2,1)}, u32[]{:S(2)}, u32[]{:S(2)}) collective-permute-start(bf16[32,64,128]{2,1,0:T(8,128)(2,1)} %fusion.145), channel_id=1, source_target_pairs={{1,0},{2,1},{3,2},{4,3},{5,4},{6,5},{7,6},{9,8},{10,9},{11,10},{12... | collective-permute-start | bytes 1572872 | tf_op jit(solution)/shard_map/while/body/eval_jaxpr/ppermute | solution.py:48
  402.0 10.8 %collective-permute-start.1 = (bf16[32,64,128]{2,1,0:T(8,128)(2,1)}, bf16[32,64,128]{2,1,0:T(8,128)(2,1)}, u32[]{:S(2)}, u32[]{:S(2)}) collective-permute-start(bf16[32,64,128]{2,1,0:T(8,128)(2,1)} %fusion.145), channel_id=1, source_target_pairs={{1,0},{2,1},{3,2},{4,3},{5,4},{6,5},{7,6},{9,8},{10,9},{11,10},{12... | collective-permute-start | bytes 1572872 | tf_op jit(solution)/shard_map/while/body/eval_jaxpr/ppermute | solution.py:48
  416.2 10.8 %collective-permute-start.1 = (bf16[32,64,128]{2,1,0:T(8,128)(2,1)}, bf16[32,64,128]{2,1,0:T(8,128)(2,1)}, u32[]{:S(2)}, u32[]{:S(2)}) collective-permute-start(bf16[32,64,128]{2,1,0:T(8,128)(2,1)} %fusion.145), channel_id=1, source_target_pairs={{1,0},{2,1},{3,2},{4,3},{5,4},{6,5},{7,6},{9,8},{10,9},{11,10},{12... | collective-permute-start | bytes 1572872 | tf_op jit(solution)/shard_map/while/body/eval_jaxpr/ppermute | solution.py:48
  442.8 12.4 %copy-start.58 = (f32[32,128]{1,0:T(8,128)S(1)}, f32[32,128]{1,0:T(8,128)}, u32[]{:S(2)}) copy-start(f32[32,128]{1,0:T(8,128)} %copy.214) | copy-start | bytes 49156
  484.0 10.1 %collective-permute-start.3 = (f32[3,2304]{1,0:T(4,128)}, f32[3,2304]{1,0:T(4,128)}, u32[]{:S(2)}, u32[]{:S(2)}) collective-permute-start(f32[3,2304]{1,0:T(4,128)} %pad_add_fusion.1), channel_id=1, source_target_pairs={{1,0},{2,1},{3,2},{4,3},{5,4},{6,5},{7,6},{9,8},{10,9},{11,10},{12... | collective-permute-start | bytes 82952 | tf_op jit(solution)/shard_map/ppermute | solution.py:48
  485.3 201.3 %reduce-scatter.7.cloned.1.call-start = ((), (), s32[]{:S(2)}) async-start(), calls=%async_computation.7 | async-start | bytes 1433600
  487.0 7.1 copy-start.1
  487.1 7.7 %copy-start.21 = (bf16[128,2048]{1,0:T(8,128)(2,1)S(1)}, bf16[128,2048]{1,0:T(8,128)(2,1)}, u32[]{:S(2)}) copy-start(bf16[128,2048]{1,0:T(8,128)(2,1)} %get-tuple-element.479) | copy-start | bytes 1572868
  487.1 7.7 %copy-start.35 = (bf16[128,32]{1,0:T(8,128)(2,1)S(1)}, bf16[128,32]{1,0:T(8,128)(2,1)}, u32[]{:S(2)}) copy-start(bf16[128,32]{1,0:T(8,128)(2,1)} %get-tuple-element.473) | copy-start | bytes 24580
  496.1 43.5 %collective-permute-start.4 = (bf16[128,4384]{0,1:T(8,128)(2,1)S(1)}, bf16[128,4384]{0,1:T(8,128)(2,1)}, u32[]{:S(2)}, u32[]{:S(2)}) collective-permute-start(bf16[128,4384]{0,1:T(8,128)(2,1)S(1)} %copy.233), channel_id=1, source_target_pairs={{0,1},{1,2},{2,3},{3,4},{4,5},{5,6},{6,7},{7,0},{8,9},{9,10},{10,1... | collective-permute-start | bytes 3366920 | tf_op jit(solution)/shard_map/ppermute | solution.py:33
  498.8 49.8 %collective-permute-start.5 = (bf16[128,4384]{0,1:T(8,128)(2,1)S(1)}, bf16[128,4384]{0,1:T(8,128)(2,1)}, u32[]{:S(2)}, u32[]{:S(2)}) collective-permute-start(bf16[128,4384]{0,1:T(8,128)(2,1)S(1)} %copy.233), channel_id=1, source_target_pairs={{0,7},{1,0},{2,1},{3,2},{4,3},{5,4},{6,5},{7,6},{8,15},{9,8},{10,9... | collective-permute-start | bytes 3366920 | tf_op jit(solution)/shard_map/ppermute | solution.py:38
  504.6 4.2 copy-start.49
  504.6 4.2 copy-start.48
  504.6 4.2 copy-start.5
  504.6 4.2 copy-start.15
  539.5 36.1 %collective-permute-start.6 = (bf16[128,4384]{0,1:T(8,128)(2,1)}, bf16[128,4384]{0,1:T(8,128)(2,1)S(1)}, u32[]{:S(2)}, u32[]{:S(2)}) collective-permute-start(bf16[128,4384]{0,1:T(8,128)(2,1)} %collective-permute-done.4), channel_id=1, source_target_pairs={{0,1},{1,2},{2,3},{3,4},{4,5},{5,6},{6,7},{7,0},{8,9},{9,10},{10,1... | collective-permute-start | bytes 3366920 | tf_op jit(solution)/shard_map/ppermute | solution.py:33
  548.6 33.5 %collective-permute-start.7 = (bf16[128,4384]{0,1:T(8,128)(2,1)}, bf16[128,4384]{0,1:T(8,128)(2,1)S(1)}, u32[]{:S(2)}, u32[]{:S(2)}) collective-permute-start(bf16[128,4384]{0,1:T(8,128)(2,1)} %collective-permute-done.5), channel_id=1, source_target_pairs={{0,7},{1,0},{2,1},{3,2},{4,3},{5,4},{6,5},{7,6},{8,15},{9,8},{10,9... | collective-permute-start | bytes 3366920 | tf_op jit(solution)/shard_map/ppermute | solution.py:38
  575.6 23.5 %collective-permute-start.8 = (bf16[128,4384]{0,1:T(8,128)(2,1)S(1)}, bf16[128,4384]{0,1:T(8,128)(2,1)S(1)}, u32[]{:S(2)}, u32[]{:S(2)}) collective-permute-start(bf16[128,4384]{0,1:T(8,128)(2,1)S(1)} %collective-permute-done.6), channel_id=1, source_target_pairs={{0,1},{1,2},{2,3},{3,4},{4,5},{5,6},{6,7},{7,0},{8,9},{9,10},{10,1... | collective-permute-start | bytes 3366920 | tf_op jit(solution)/shard_map/ppermute | solution.py:33
  582.1 25.9 %collective-permute-start.9 = (bf16[128,4384]{0,1:T(8,128)(2,1)S(1)}, bf16[128,4384]{0,1:T(8,128)(2,1)S(1)}, u32[]{:S(2)}, u32[]{:S(2)}) collective-permute-start(bf16[128,4384]{0,1:T(8,128)(2,1)S(1)} %collective-permute-done.7), channel_id=1, source_target_pairs={{0,7},{1,0},{2,1},{3,2},{4,3},{5,4},{6,5},{7,6},{8,15},{9,8},{10,9... | collective-permute-start | bytes 3366920 | tf_op jit(solution)/shard_map/ppermute | solution.py:38
  599.0 20.8 %collective-permute-start.10 = (bf16[128,4384]{0,1:T(8,128)(2,1)S(1)}, bf16[128,4384]{0,1:T(8,128)(2,1)S(1)}, u32[]{:S(2)}, u32[]{:S(2)}) collective-permute-start(bf16[128,4384]{0,1:T(8,128)(2,1)S(1)} %collective-permute-done.8), channel_id=1, source_target_pairs={{0,1},{1,2},{2,3},{3,4},{4,5},{5,6},{6,7},{7,0},{8,9},{9,10},{10,1... | collective-permute-start | bytes 3366920 | tf_op jit(solution)/shard_map/ppermute | solution.py:33
  625.3 86.8 %reduce-scatter.9.cloned.1.call-start = ((), (), s32[]{:S(2)}) async-start(), calls=%async_computation.8 | async-start | bytes 655360
  626.2 6.9 copy-start.52
  626.2 6.9 copy-start.55
  626.2 6.9 copy-start.74
  626.2 54.6 %copy-start.76 = (f32[128]{0:T(128)S(1)}, f32[128]{0:T(128)}, u32[]{:S(2)}) copy-start(f32[128]{0:T(128)} %copy-done.75) | copy-start | bytes 1540
  626.2 54.6 %copy-start.23 = (f32[1,128,1024]{2,1,0:T(8,128)S(1)}, f32[1,128,1024]{2,1,0:T(8,128)}, u32[]{:S(2)}) copy-start(f32[1,128,1024]{2,1,0:T(8,128)} %param.17) | copy-start | bytes 1572868
  633.1 48.7 %copy-start.45 = (f32[14688]{0:T(1024)S(1)}, f32[14688]{0:T(1024)}, u32[]{:S(2)}) copy-start(f32[14688]{0:T(1024)} %param.26) | copy-start | bytes 176260
  633.1 48.7 %copy-start.46 = (f32[14688]{0:T(1024)S(1)}, f32[14688]{0:T(1024)}, u32[]{:S(2)}) copy-start(f32[14688]{0:T(1024)} %param.27) | copy-start | bytes 176260
  686.5 25.6 %copy-start.25 = (f32[32,2048]{1,0:T(8,128)S(1)}, f32[32,2048]{1,0:T(8,128)}, u32[]{:S(2)}) copy-start(f32[32,2048]{1,0:T(8,128)} %param.20) | copy-start | bytes 786436
  686.5 25.6 %copy-start.30 = (f32[32,2048]{1,0:T(8,128)S(1)}, f32[32,2048]{1,0:T(8,128)}, u32[]{:S(2)}) copy-start(f32[32,2048]{1,0:T(8,128)} %param.23) | copy-start | bytes 786436
  686.5 25.6 %copy-start.31 = (f32[32,2048]{1,0:T(8,128)S(1)}, f32[32,2048]{1,0:T(8,128)}, u32[]{:S(2)}) copy-start(f32[32,2048]{1,0:T(8,128)} %param.24) | copy-start | bytes 786436
  (45 other events, 102.9 us)
Sparse Core Ops, SparseCore 0:
  11.4 82.9 all-gather.5
  98.1 60.2 all-gather.7
  160.5 34.3 all-gather.9
  197.0 34.3 all-gather.11
  485.4 81.0 all-gather.13
  625.4 35.7 reduce-scatter.6
  686.6 25.4 reduce-scatter.8
